TPU v7x, 128 devices: a whole 4x4x4 slice. The times are simulated.
128 devices in a mesh: ctx: 16 (over z_hi, x, core), head: 8 (over z_lo, y).
Axes of the slice: x: 4, y: 4, z: 4 (z_hi: 2, z_lo: 2; z = z_hi * 2 + z_lo), core: 2. Of those that a mesh axis runs over, the one named last changes fastest.
Arguments:
- tokens: bfloat16 [16384, 4096], P('ctx', 'head'), may hold values from -23 to 23
- proj_weight: bfloat16 [4096, 32, 384], P(None, 'head'), may hold values from -1 to 1
- partner_shard: int32 [32, 256, 3], P('head'), may hold values from 0 to 15, all different within a row; in each aligned block of 16 rows (0 to 15, 16 to 31, ..., all dimensions but the last counted through in order) at most 6 rows name the same one
- partner_block: int32 [32, 256, 3], P('head'), may hold values from 0 to 15
Outputs:
- attended: bfloat16 [16384, 32, 128], P('ctx', 'head')
Inputs may be any that keep to these rules, and one draw needn't show every extreme that they name: `partner_shard`: the 3 entries of one row differ. For each head, within each aligned run of 16 block rows, no value is named more than 6 times, and some runs name one value exactly 6 times.
All inputs are finite; a program needn't handle non-finite values.
Results may differ from a plain program's by a relative error of at most 0.008.
Values may be sent and summed in bfloat16 or wider, within the bound.
A program may use at most 192 MiB of HBM per device.

v0:
```python
import jax
import jax.numpy as jnp
from jax import lax
from jax.sharding import PartitionSpec as P

HEAD_DIMENSION = 128
BLK = 64
GLOB = 2
RAND = 3


def padded_2(cells, sides, width):
    for axis, dim in sides:
        count = lax.axis_size(axis)
        head = lax.slice_in_dim(cells, 0, width, axis=dim)
        tail = lax.slice_in_dim(cells, cells.shape[dim] - width, cells.shape[dim], axis=dim)
        cells = jnp.concatenate(
            [
                lax.ppermute(tail, axis, [(i, (i + 1) % count) for i in range(count)]),
                cells,
                lax.ppermute(head, axis, [((i + 1) % count, i) for i in range(count)]),
            ],
            axis=dim,
        )
    return cells


def from_root(block, axis, holder):
    block = jnp.where(lax.axis_index(axis) == holder, block, jnp.zeros_like(block))
    return lax.psum(block, axis)


def combined_all(part, axis, combine):
    gathered = jax.tree.map(lambda a: lax.all_gather(a, axis), part)

    def take(source):
        return jax.tree.map(lambda a: lax.dynamic_index_in_dim(a, source, 0, False), gathered)

    return lax.fori_loop(
        1, lax.axis_size(axis), lambda source, state: combine(state, take(source)), take(0)
    )


def per_device(tokens, proj_weight, partner_shard, partner_block):
    row_count = tokens.shape[0]
    head_count = proj_weight.shape[1]
    blocks = row_count // BLK
    shard_index = lax.axis_index("ctx")
    inverse_root_scale = HEAD_DIMENSION ** (-0.5)
    packed = jnp.einsum(
        "td,dhe->the",
        lax.all_gather(tokens, "head", axis=1, tiled=True),
        proj_weight,
        preferred_element_type=jnp.float32,
    ).astype(jnp.bfloat16)
    queries = packed[..., :HEAD_DIMENSION]
    keyval = packed[..., HEAD_DIMENSION:]
    padded = padded_2(keyval, (("ctx", 0),), BLK)
    window = jnp.concatenate(
        [
            padded[0:row_count].reshape(blocks, BLK, head_count, 2 * HEAD_DIMENSION),
            padded[BLK : row_count + BLK].reshape(blocks, BLK, head_count, 2 * HEAD_DIMENSION),
            padded[2 * BLK : row_count + 2 * BLK].reshape(
                blocks, BLK, head_count, 2 * HEAD_DIMENSION
            ),
        ],
        axis=1,
    )
    global_pack = from_root(packed[: GLOB * BLK], "ctx", 0)
    global_query = global_pack[..., :HEAD_DIMENSION]
    global_keyval = global_pack[..., HEAD_DIMENSION:]
    row_total = blocks * RAND
    owners = lax.dynamic_slice_in_dim(partner_shard, shard_index * blocks, blocks, 1).reshape(
        head_count, row_total
    )
    offsets = lax.dynamic_slice_in_dim(partner_block, shard_index * blocks, blocks, 1).reshape(
        head_count, row_total
    )
    partner_index = owners * blocks + offsets
    block_rows = lax.all_gather(keyval, "ctx", axis=0, tiled=True)
    piece_blocks = block_rows.shape[0] // BLK
    piece_hot = (partner_index[..., None] == jnp.arange(piece_blocks)).astype(jnp.bfloat16)
    blocked = block_rows.reshape(piece_blocks, BLK, head_count, 2 * HEAD_DIMENSION)
    fetched = jnp.einsum(
        "hrb,bthe->hrte", piece_hot, blocked, preferred_element_type=jnp.float32
    ).astype(jnp.bfloat16)
    remote = fetched
    remote = remote.reshape(head_count, blocks, RAND * BLK, 2 * HEAD_DIMENSION)
    blocked_query_rows = queries.reshape(blocks, BLK, head_count, HEAD_DIMENSION)
    window_scores = jnp.einsum(
        "bqhd,bkhd->bhqk",
        blocked_query_rows,
        window[..., :HEAD_DIMENSION],
        preferred_element_type=jnp.float32,
    )
    global_scores = jnp.einsum(
        "bqhd,khd->bhqk",
        blocked_query_rows,
        global_keyval[..., :HEAD_DIMENSION],
        preferred_element_type=jnp.float32,
    )
    remote_scores = jnp.einsum(
        "bqhd,hbkd->bhqk",
        blocked_query_rows,
        remote[..., :HEAD_DIMENSION],
        preferred_element_type=jnp.float32,
    )
    logit_scores = (
        jnp.concatenate([window_scores, global_scores, remote_scores], axis=-1) * inverse_root_scale
    )
    softmax_weight_matrix = jax.nn.softmax(logit_scores, axis=-1).astype(jnp.bfloat16)
    width_window = 3 * BLK
    width_global = GLOB * BLK
    context = jnp.einsum(
        "bhqk,bkhd->bqhd",
        softmax_weight_matrix[..., :width_window],
        window[..., HEAD_DIMENSION:],
        preferred_element_type=jnp.float32,
    )
    context = context + jnp.einsum(
        "bhqk,khd->bqhd",
        softmax_weight_matrix[..., width_window : width_window + width_global],
        global_keyval[..., HEAD_DIMENSION:],
        preferred_element_type=jnp.float32,
    )
    context = context + jnp.einsum(
        "bhqk,hbkd->bqhd",
        softmax_weight_matrix[..., width_window + width_global :],
        remote[..., HEAD_DIMENSION:],
        preferred_element_type=jnp.float32,
    )
    sparse_attention_output = context.astype(jnp.bfloat16).reshape(
        row_count, head_count, HEAD_DIMENSION
    )
    lead_scores = (
        jnp.einsum(
            "qhd,khd->hqk",
            global_query,
            keyval[..., :HEAD_DIMENSION],
            preferred_element_type=jnp.float32,
        )
        * inverse_root_scale
    )
    maxima = jnp.max(lead_scores, axis=-1)
    exp_terms = jnp.exp(lead_scores - maxima[..., None])
    totals = jnp.sum(exp_terms, axis=-1)
    summed = jnp.einsum(
        "hqk,khd->hqd",
        exp_terms,
        keyval[..., HEAD_DIMENSION:].astype(jnp.float32),
        precision=lax.Precision.HIGHEST,
    )

    def combine(first, second):
        max_first, total_first, sum_first = first
        max_second, total_second, sum_second = second
        larger = jnp.maximum(max_first, max_second)
        factor_first = jnp.exp(max_first - larger)
        factor_second = jnp.exp(max_second - larger)
        return (
            larger,
            total_first * factor_first + total_second * factor_second,
            sum_first * factor_first[..., None] + sum_second * factor_second[..., None],
        )

    maxima, totals, summed = combined_all((maxima, totals, summed), "ctx", combine)
    global_out = jnp.transpose((summed / totals[..., None]).astype(jnp.bfloat16), (1, 0, 2))
    head_rows = jnp.where(shard_index == 0, global_out, sparse_attention_output[: GLOB * BLK])
    return jnp.concatenate([head_rows, sparse_attention_output[GLOB * BLK :]], axis=0)


def solution(mesh):
    in_specs = (
        P("ctx", "head"),
        P(None, "head", None),
        P("head", None, None),
        P("head", None, None),
    )
    out_specs = P("ctx", "head", None)
    return jax.shard_map(
        per_device, mesh=mesh, in_specs=in_specs, out_specs=out_specs, check_vma=False
    )
```

profile of v0, /device:TPU:1, one launch (start us, length us, event | category | flops | bytes accessed | tf_op | source)
XLA Modules:
  0.0 600.8 jit_solution(12266525961735290425)
XLA Ops:
  6.5 0.7 all-gather.9.cloned.1.call-update
  7.3 0.0 all-reduce.2.cloned.1.call-start
  7.3 96.7 %all-gather.9.cloned.1.call-done = bf16[1024,4096]{1,0:T(8,128)(2,1)} async-done(((bf16[1024,512]{1,0:T(8,128)(2,1)}), bf16[1024,4096]{1,0:T(8,128)(2,1)}) %all-gather.9.cloned.1.call-update) | async-done | bytes 8388624 | tf_op jit(solution)/shard_map/all_gather | solution.py:52
  104.0 18.3 %fusion.22 = bf16[1024,4,384]{2,0,1:T(8,128)(2,1)S(1)} fusion(bf16[4096,4,384]{2,1,0:T(4,128)(2,1)} %param.7, bf16[1024,4096]{1,0:T(8,128)(2,1)} %all-gather.9.cloned.1.call-done), kind=kOutput, calls=%fused_computation.29 | convolution fusion | flops 12886474752 | bytes 24117248 | tf_op jit(solution)/shard_map/td,dhe->the/dot_general | solution.py:50
  122.3 0.8 slice_select_fusion
  123.2 0.0 all-reduce.2.cloned.1.call-update
  123.2 0.0 all-gather.13.cloned.1.call-start
  123.2 138.2 %all-reduce.2.cloned.1.call-done = bf16[128,4,384]{2,0,1:T(8,128)(2,1)} async-done(((bf16[128,4,384]{2,0,1:T(8,128)(2,1)}), bf16[128,4,384]{2,0,1:T(8,128)(2,1)}) %all-reduce.2.cloned.1.call-update) | async-done | bytes 393232 | tf_op jit(solution)/shard_map/psum | solution.py:30
  261.4 1.4 multiply_reduce_fusion
  262.8 1.3 copy-done.1
  264.1 2.2 fusion.30
  266.3 0.0 all-gather.13.cloned.1.call-update
  266.3 0.0 all-gather.11.cloned.1.call-start
  266.4 1.5 slice.118
  267.9 0.0 all-gather.11.cloned.1.call-update
  267.9 1.8 fusion.56
  269.7 0.7 collective-permute-start.1
  270.4 0.8 dynamic-slice_add_fusion
  271.1 0.1 copy.40
  271.2 0.1 add.84
  271.3 1.3 slice.116
  272.6 1.4 collective-permute-done.1
  274.1 0.3 pad_maximum_fusion.2
  274.4 5.0 pad_maximum_fusion
  279.4 3.4 fusion.54
  282.8 4.1 fusion.20
  286.9 25.5 %all-gather.3 = f32[16,4,128]{2,1,0:T(4,128)S(1)} all-gather(f32[1,4,128]{2,1,0:T(4,128)S(1)} %bitcast.75), channel_id=2, replica_groups=mesh['ctx'=16,'head'=8] {'ctx'}, dimensions={0}, use_global_device_ids=true | all-gather | bytes 34816 | tf_op jit(solution)/shard_map/all_gather | solution.py:34
  312.4 0.5 fusion.31
  312.9 19.5 %all-gather.4 = f32[16,4,128]{2,1,0:T(4,128)S(1)} all-gather(f32[1,4,128]{2,1,0:T(4,128)S(1)} %bitcast.76), channel_id=3, replica_groups=mesh['ctx'=16,'head'=8] {'ctx'}, dimensions={0}, use_global_device_ids=true | all-gather | bytes 34816 | tf_op jit(solution)/shard_map/all_gather | solution.py:34
  332.4 1.3 convolution_bitcast_fusion
  333.7 0.0 all-gather.13.cloned.1.call-done
  333.8 1.0 slice.115
  334.8 19.0 %while.19 = (s32[]{:T(128)}, f32[4,128]{1,0:T(4,128)S(1)}, f32[4,128]{1,0:T(4,128)S(1)}, f32[4,128,128]{2,1,0:T(8,128)S(1)}, f32[16,4,128]{2,1,0:T(4,128)S(1)}, ...) while((s32[]{:T(128)}, f32[4,128]{1,0:T(4,128)S(1)}, ...), condition=%wide.region_4.5_spmd, body=%wide.region_3.4_spmd.sunk | while | flops 199685 | bytes 807063 | solution.py:39
  334.8 1.3 fusion.61
  336.1 1.2 fusion.61
  337.4 1.2 fusion.61
  338.7 1.3 fusion.61
  340.0 1.2 fusion.61
  341.2 1.2 fusion.61
  342.5 1.2 fusion.61
  343.8 1.2 fusion.61
  345.0 1.2 fusion.61
  346.3 1.2 fusion.61
  347.5 1.2 fusion.61
  348.8 1.2 fusion.61
  350.1 1.2 fusion.61
  351.3 1.2 fusion.61
  352.6 1.2 fusion.61
  353.8 158.4 %all-gather.11.cloned.1.call-done = bf16[16384,4,256]{2,0,1:T(8,128)(2,1)} async-done(((bf16[1024,4,256]{2,0,1:T(8,128)(2,1)}), bf16[16384,4,256]{2,0,1:T(8,128)(2,1)}) %all-gather.11.cloned.1.call-update) | async-done | bytes 33554448 | tf_op jit(solution)/shard_map/all_gather | solution.py:80
  512.2 34.4 %fusion.11 = bf16[4,48,64,256]{3,1,2,0:T(8,128)(2,1)S(1)} fusion(bf16[256,64,4,256]{3,1,0,2:T(8,128)(2,1)} %bitcast.65, s32[4,48]{1,0:T(4,128)S(1)} %add.84), kind=kOutput, calls=%fused_computation.20 | convolution fusion | flops 1613807616 | bytes 39846656 | tf_op jit(solution)/shard_map/hrb,bthe->hrte/dot_general | solution.py:84
  546.6 2.5 copy.42
  549.1 1.8 fusion.55
  550.9 4.1 fusion.18
  555.0 28.1 %fusion.57 = (f32[16,4,64]{2,1,0:T(4,128)S(1)}, f32[16,4,64,512]{3,2,1,0:T(8,128)}) fusion(f32[16,4,64,192]{3,2,1,0:T(8,128)} %fusion.18, f32[16,4,64,128]{3,2,1,0:T(8,128)S(1)} %convolution_bitcast_fusion, f32[16,4,64,192]{3,2,1,0:T(8,128)S(1)} %copy-done.5), kind=kOutput, calls=%fused_computation.71 | output fusion | flops 10486271 | bytes 16793600 | tf_op jit(solution)/shard_map/sub | solution.py:111
  583.1 4.1 divide_convert_fusion
  587.1 1.3 fusion.14
  588.4 1.6 fusion.36
  590.0 0.4 copy-done.3
  590.4 1.4 fusion.29
  591.8 0.1 slice.130
  591.9 0.1 copy.47
  592.0 0.1 bitcast_select_fusion
  592.1 0.1 pad_maximum_fusion.3
  592.2 1.8 copy.48
  (32 shorter events, 0.4 us)
Async XLA Ops:
  6.5 97.4 %all-gather.9.cloned.1.call-start = ((), (), s32[]{:S(2)}) async-start(), calls=%async_computation | async-start | bytes 9437184 | tf_op jit(solution)/shard_map/all_gather | solution.py:52
  7.3 254.2 %all-reduce.2.cloned.1.call-start = ((), (), s32[]{:S(2)}) async-start(), calls=%async_computation.1 | async-start | bytes 786432 | tf_op jit(solution)/shard_map/psum | solution.py:30
  122.3 144.1 %copy-start.4 = (bf16[1024,4,384]{2,0,1:T(8,128)(2,1)}, bf16[1024,4,384]{2,0,1:T(8,128)(2,1)S(1)}, u32[]{:S(2)}) copy-start(bf16[1024,4,384]{2,0,1:T(8,128)(2,1)S(1)} %fusion.22) | copy-start | bytes 9437188
  123.2 210.6 %all-gather.13.cloned.1.call-start = ((), (), s32[]{:S(2)}) async-start(), calls=%async_computation.3 | async-start | bytes 4456448 | tf_op jit(solution)/shard_map/all_gather | solution.py:34
  262.8 1.3 copy-start.1
  266.3 245.9 %all-gather.11.cloned.1.call-start = ((), (), s32[]{:S(2)}) async-start(), calls=%async_computation.2 | async-start | bytes 35651584 | tf_op jit(solution)/shard_map/all_gather | solution.py:80
  267.9 6.2 %copy-start = (bf16[1024,4,256]{2,0,1:T(8,128)(2,1)S(1)}, bf16[1024,4,256]{2,0,1:T(8,128)(2,1)}, u32[]{:S(2)}) copy-start(bf16[1024,4,256]{2,0,1:T(8,128)(2,1)} %slice.118) | copy-start | bytes 6291460
  269.7 2.9 collective-permute-start
  269.7 4.4 collective-permute-start.1
  282.8 29.6 %copy-start.2 = (f32[4,128,1024]{2,1,0:T(8,128)S(1)}, f32[4,128,1024]{2,1,0:T(8,128)}, u32[]{:S(2)}) copy-start(f32[4,128,1024]{2,1,0:T(8,128)} %copy-done.1) | copy-start | bytes 6291460
  550.9 4.1 copy-start.5
  588.4 2.0 copy-start.3
Sparse Core Ops, SparseCore 0:
  9.0 94.9 all-gather.8
  123.3 138.0 all-reduce.1
  266.4 57.4 all-gather.12
  326.3 185.8 all-gather.10
where the time goes:
time: 610 us; the launch traced here: 601 us
  waiting for transfers between devices  396 us (65%)
  matrix products  70 us (11%)
  other arithmetic  58.3 us (10%)
  blocking collectives  45 us (7%)
  local copies, waits for them, and re-layouts  17.1 us (3%)
  between operations  13.6 us (2%)
    all_gather x1, waiting for transfers between devices, per_device(): block_rows = lax.all_gather(keyval, 'ctx', axis=0, tiled=True)  158 us
    psum x1, waiting for transfers between devices, from_root(): return lax.psum(block, axis)  138 us
    all_gather x1, waiting for transfers between devices, per_device(): lax.all_gather(tokens, 'head', axis=1, tiled=True)  96.7 us
    all_gather x2, blocking collectives, combined_all(): gathered = jax.tree.map(lambda a: lax.all_gather(a, axis), part)  45 us
    dot_general x1, matrix products, per_device(): jnp.einsum('hrb,bthe->hrte', piece_hot, blocked, preferred_element_type=j...  34.4 us
    sub x1, other arithmetic, per_device(): jax.nn.softmax(logit_scores, axis=-1).astype(jnp.bfloat16)  28.1 us
    dot_general x1, matrix products, per_device(): jnp.einsum('td,dhe->the', lax.all_gather(tokens, 'head', axis=1, tiled=Tr...  18.3 us
    add x15, other arithmetic, combine(): sum_first * factor_first[..., None] + sum_second * factor_second[..., None]  18.2 us
  transfers between devices with their start and end apart: 6, of which 4 were waited for; matrix products, arithmetic and copies ran while one was open for 7% of the time, Pallas kernels for 0%

commit v1 on v0

--- a/solution.py
+++ b/solution.py
@@ -27,7 +27,7 @@
 
 def from_root(block, axis, holder):
     block = jnp.where(lax.axis_index(axis) == holder, block, jnp.zeros_like(block))
-    return lax.psum(block, axis)
+    return jnp.sum(lax.all_gather(block, axis), axis=0)
 
 
 def combined_all(part, axis, combine):

time: 610 us -> 534 us (0.88)
  waiting for transfers between devices: 396 us -> 319 us
    psum x1 -> x0, waiting for transfers between devices: 138 us -> none  [from_root(): return lax.psum(block, axis)]
    all_gather x0 -> x1, waiting for transfers between devices: none -> 63.2 us  [from_root(): return jnp.sum(lax.all_gather(block, axis), axis=0)]
  transfers between devices with their start and end apart: 6 -> 6, of which waited for: 4 -> 4; matrix products, arithmetic and copies ran while one was open for 7% -> 8% of each run, Pallas kernels for 0% -> 0%
where the time goes in v1:
time: 534 us; the launch traced here: 527 us
  waiting for transfers between devices  319 us (60%)
  matrix products  69 us (13%)
  other arithmetic  62.2 us (12%)
  blocking collectives  44.1 us (8%)
  local copies, waits for them, and re-layouts  17.4 us (3%)
  between operations  13.6 us (3%)
    all_gather x1, waiting for transfers between devices, per_device(): block_rows = lax.all_gather(keyval, 'ctx', axis=0, tiled=True)  156 us
    all_gather x1, waiting for transfers between devices, per_device(): lax.all_gather(tokens, 'head', axis=1, tiled=True)  96.7 us
    all_gather x1, waiting for transfers between devices, from_root(): return jnp.sum(lax.all_gather(block, axis), axis=0)  63.2 us
    all_gather x2, blocking collectives, combined_all(): gathered = jax.tree.map(lambda a: lax.all_gather(a, axis), part)  44.1 us
    dot_general x1, matrix products, per_device(): jnp.einsum('hrb,bthe->hrte', piece_hot, blocked, preferred_element_type=j...  34.4 us
    sub x1, other arithmetic, per_device(): jax.nn.softmax(logit_scores, axis=-1).astype(jnp.bfloat16)  28.1 us
    dot_general x1, matrix products, per_device(): jnp.einsum('td,dhe->the', lax.all_gather(tokens, 'head', axis=1, tiled=Tr...  18.3 us
    add x15, other arithmetic, combine(): sum_first * factor_first[..., None] + sum_second * factor_second[..., None]  18.2 us
  transfers between devices with their start and end apart: 6, of which 4 were waited for; matrix products, arithmetic and copies ran while one was open for 8% of the time, Pallas kernels for 0%

profile of v1, /device:TPU:1, one launch (start us, length us, event | category | flops | bytes accessed | tf_op | source)
XLA Modules:
  0.0 527.0 jit_solution(959025131136193785)
XLA Ops:
  6.5 0.7 all-gather.11.cloned.1.call-update
  7.3 0.0 all-gather.15.cloned.1.call-start
  7.3 96.7 %all-gather.11.cloned.1.call-done = bf16[1024,4096]{1,0:T(8,128)(2,1)} async-done(((bf16[1024,512]{1,0:T(8,128)(2,1)}), bf16[1024,4096]{1,0:T(8,128)(2,1)}) %all-gather.11.cloned.1.call-update) | async-done | bytes 8388624 | tf_op jit(solution)/shard_map/all_gather | solution.py:52
  104.0 18.3 %fusion.22 = bf16[1024,4,384]{2,0,1:T(8,128)(2,1)S(1)} fusion(bf16[4096,4,384]{2,1,0:T(4,128)(2,1)} %param.7, bf16[1024,4096]{1,0:T(8,128)(2,1)} %all-gather.11.cloned.1.call-done), kind=kOutput, calls=%fused_computation.29 | convolution fusion | flops 12886474752 | bytes 24117248 | tf_op jit(solution)/shard_map/td,dhe->the/dot_general | solution.py:50
  122.3 0.9 slice_select_fusion
  123.2 0.0 all-gather.17.cloned.1.call-start
  123.2 63.2 %all-gather.15.cloned.1.call-done = bf16[2048,4,384]{2,0,1:T(8,128)(2,1)} async-done(((bf16[128,4,384]{2,0,1:T(8,128)(2,1)}), bf16[2048,4,384]{2,0,1:T(8,128)(2,1)}) %all-gather.15.cloned.1.call-update) | async-done | bytes 6291472 | tf_op jit(solution)/shard_map/all_gather | solution.py:30
  186.4 3.9 reduce_sum.30
  190.4 0.5 multiply_reduce_fusion
  190.9 1.3 copy-done.1
  192.2 2.2 fusion.30
  194.3 0.0 all-gather.17.cloned.1.call-update
  194.4 0.0 all-gather.13.cloned.1.call-start
  194.4 1.5 slice.118
  196.0 1.8 fusion.56
  197.8 0.9 collective-permute-start
  198.7 0.3 collective-permute-start.1
  199.0 0.8 dynamic-slice_add_fusion
  199.8 0.1 copy.40
  199.9 0.1 add.82
  200.0 1.3 slice.116
  201.3 2.1 collective-permute-done.1
  203.4 0.3 pad_maximum_fusion.2
  203.7 5.0 pad_maximum_fusion
  208.7 3.4 fusion.54
  212.1 4.1 fusion.20
  216.2 24.3 %all-gather.4 = f32[16,4,128]{2,1,0:T(4,128)S(1)} all-gather(f32[1,4,128]{2,1,0:T(4,128)S(1)} %bitcast.77), channel_id=3, replica_groups=mesh['ctx'=16,'head'=8] {'ctx'}, dimensions={0}, use_global_device_ids=true | all-gather | bytes 34816 | tf_op jit(solution)/shard_map/all_gather | solution.py:34
  240.4 0.5 fusion.31
  240.9 19.9 %all-gather.5 = f32[16,4,128]{2,1,0:T(4,128)S(1)} all-gather(f32[1,4,128]{2,1,0:T(4,128)S(1)} %bitcast.78), channel_id=4, replica_groups=mesh['ctx'=16,'head'=8] {'ctx'}, dimensions={0}, use_global_device_ids=true | all-gather | bytes 34816 | tf_op jit(solution)/shard_map/all_gather | solution.py:34
  260.8 1.4 convolution_bitcast_fusion
  262.2 0.0 all-gather.17.cloned.1.call-done
  262.2 1.0 slice.115
  263.2 18.9 %while.19 = (s32[]{:T(128)}, f32[4,128]{1,0:T(4,128)S(1)}, f32[4,128]{1,0:T(4,128)S(1)}, f32[4,128,128]{2,1,0:T(8,128)S(1)}, f32[16,4,128]{2,1,0:T(4,128)S(1)}, ...) while((s32[]{:T(128)}, f32[4,128]{1,0:T(4,128)S(1)}, ...), condition=%wide.region_4.5_spmd, body=%wide.region_3.4_spmd.sunk | while | flops 199685 | bytes 807063 | solution.py:39
  263.3 1.2 fusion.61
  264.6 1.3 fusion.61
  265.9 1.2 fusion.61
  267.1 1.2 fusion.61
  268.4 1.2 fusion.61
  269.6 1.2 fusion.61
  270.9 1.2 fusion.61
  272.2 1.2 fusion.61
  273.4 1.2 fusion.61
  274.7 1.2 fusion.61
  275.9 1.2 fusion.61
  277.2 1.2 fusion.61
  278.4 1.2 fusion.61
  279.7 1.2 fusion.61
  281.0 1.2 fusion.61
  282.2 156.3 %all-gather.13.cloned.1.call-done = bf16[16384,4,256]{2,0,1:T(8,128)(2,1)} async-done(((bf16[1024,4,256]{2,0,1:T(8,128)(2,1)}), bf16[16384,4,256]{2,0,1:T(8,128)(2,1)}) %all-gather.13.cloned.1.call-update) | async-done | bytes 33554448 | tf_op jit(solution)/shard_map/all_gather | solution.py:80
  438.4 34.4 %fusion.11 = bf16[4,48,64,256]{3,1,2,0:T(8,128)(2,1)S(1)} fusion(bf16[256,64,4,256]{3,1,0,2:T(8,128)(2,1)} %bitcast.66, s32[4,48]{1,0:T(4,128)S(1)} %add.82), kind=kOutput, calls=%fused_computation.20 | convolution fusion | flops 1613807616 | bytes 39846656 | tf_op jit(solution)/shard_map/hrb,bthe->hrte/dot_general | solution.py:84
  472.8 2.5 copy.42
  475.3 1.8 fusion.55
  477.1 4.1 fusion.18
  481.2 28.1 %fusion.57 = (f32[16,4,64]{2,1,0:T(4,128)S(1)}, f32[16,4,64,512]{3,2,1,0:T(8,128)}) fusion(f32[16,4,64,192]{3,2,1,0:T(8,128)} %fusion.18, f32[16,4,64,128]{3,2,1,0:T(8,128)S(1)} %convolution_bitcast_fusion, f32[16,4,64,192]{3,2,1,0:T(8,128)S(1)} %copy-done.5), kind=kOutput, calls=%fused_computation.71 | output fusion | flops 10486271 | bytes 16793600 | tf_op jit(solution)/shard_map/sub | solution.py:111
  509.3 4.1 divide_convert_fusion
  513.3 1.4 fusion.36
  514.8 1.3 fusion.14
  516.0 0.6 copy-done.3
  516.6 1.4 fusion.29
  518.1 0.1 slice.130
  518.2 0.1 copy.47
  518.3 0.1 bitcast_select_fusion
  518.4 0.1 pad_maximum_fusion.3
  518.5 1.8 copy.48
  (35 shorter events, 0.5 us)
Async XLA Ops:
  6.5 97.4 %all-gather.11.cloned.1.call-start = ((), (), s32[]{:S(2)}) async-start(), calls=%async_computation | async-start | bytes 9437184 | tf_op jit(solution)/shard_map/all_gather | solution.py:52
  7.3 179.2 %all-gather.15.cloned.1.call-start = ((), (), s32[]{:S(2)}) async-start(), calls=%async_computation.2 | async-start | bytes 6684672 | tf_op jit(solution)/shard_map/all_gather | solution.py:30
  122.3 72.1 %copy-start.4 = (bf16[1024,4,384]{2,0,1:T(8,128)(2,1)}, bf16[1024,4,384]{2,0,1:T(8,128)(2,1)S(1)}, u32[]{:S(2)}) copy-start(bf16[1024,4,384]{2,0,1:T(8,128)(2,1)S(1)} %fusion.22) | copy-start | bytes 9437188
  123.2 139.0 %all-gather.17.cloned.1.call-start = ((), (), s32[]{:S(2)}) async-start(), calls=%async_computation.3 | async-start | bytes 4456448 | tf_op jit(solution)/shard_map/all_gather | solution.py:34
  190.4 4.0 copy-start.6
  190.9 1.3 copy-start.1
  194.4 244.1 %all-gather.13.cloned.1.call-start = ((), (), s32[]{:S(2)}) async-start(), calls=%async_computation.1 | async-start | bytes 35651584 | tf_op jit(solution)/shard_map/all_gather | solution.py:80
  195.9 7.4 %copy-start = (bf16[1024,4,256]{2,0,1:T(8,128)(2,1)S(1)}, bf16[1024,4,256]{2,0,1:T(8,128)(2,1)}, u32[]{:S(2)}) copy-start(bf16[1024,4,256]{2,0,1:T(8,128)(2,1)} %slice.118) | copy-start | bytes 6291460
  197.8 3.5 collective-permute-start
  198.7 4.7 collective-permute-start.1
  212.1 28.3 %copy-start.2 = (f32[4,128,1024]{2,1,0:T(8,128)S(1)}, f32[4,128,1024]{2,1,0:T(8,128)}, u32[]{:S(2)}) copy-start(f32[4,128,1024]{2,1,0:T(8,128)} %copy-done.1) | copy-start | bytes 6291460
  477.1 4.1 copy-start.5
  514.8 1.9 copy-start.3
Sparse Core Ops, SparseCore 0:
  9.0 94.9 all-gather.10
  123.3 63.0 all-gather.14
  194.5 55.6 all-gather.16
  252.5 185.8 all-gather.12
